TPU v7x, 32 devices: a whole 2x2x4 slice. The times are simulated.
32 devices in a mesh: clips: 2 (over y), tiles: 16 (over z, x, core).
Axes of the slice: x: 2, y: 2, z: 4, core: 2. Of those that a mesh axis runs over, the one named last changes fastest.
Arguments:
- frames: bfloat16 [4, 64, 256, 128], P(None, None, ('clips', 'tiles')), parts along dimension 2, may hold values from -6 to 6
- motion_forward: int32 [3, 512], P(None, ('clips', 'tiles')), parts along dimension 1, may hold values from 0 to 255, as said below
- motion_backward: int32 [3, 512], P(None, ('clips', 'tiles')), parts along dimension 1, may hold values from 0 to 255, as said below
- join_weight: bfloat16 [2, 64, 128], replicated, may hold values from -0.5 to 0.5
- conv_weight: bfloat16 [2, 4, 9, 64, 64], replicated, may hold values from -0.125 to 0.125
Outputs:
- forward_features: bfloat16 [4, 64, 256, 128], P(None, None, ('clips', 'tiles')), parts along dimension 2
- backward_features: bfloat16 [4, 64, 256, 128], P(None, None, ('clips', 'tiles')), parts along dimension 2
There are 2 independent parts, one for each index of `clips`. A program takes and returns all parts, laid end to end along the dimension named above; an argument that names none is the same for every part. Nothing has to cross between parts.
Inputs may be any that keep to these rules, and one draw needn't show every extreme that they name: `motion_forward`: entries are block numbers of the frame; block number k lies in rows held by device k // 16. A block of device d takes a block of a device at most 2 away from d, at most two block columns to either side of its own column. Of the 16 blocks of one device, either none or exactly 4 take blocks of any one other device; in every frame some device takes 4 blocks from each device up to 2 away on both sides. `motion_backward`: entries are block numbers of the frame; block number k lies in rows held by device k // 16. A block of device d takes a block of a device at most 2 away from d, at most two block columns to either side of its own column. Of the 16 blocks of one device, either none or exactly 4 take blocks of any one other device; in every frame some device takes 4 blocks from each device up to 2 away on both sides.
All inputs are finite; a program needn't handle non-finite values.
Results may differ from a plain program's by a relative error of at most 0.018.
Values may be sent and summed in bfloat16 or wider, within the bound.
A program may use at most 64 MiB of HBM per device.

v0:
```python
import functools

import jax
import jax.numpy as jnp
from jax import lax
from jax.experimental import pallas as pl
from jax.experimental.pallas import tpu as pltpu
from jax.sharding import PartitionSpec as P

BS = 8
REACH = 2
OFFSETS = tuple(o for o in range(-REACH, REACH + 1) if o != 0)


def leaky(value):
    return jnp.where(value >= 0, value, 0.1 * value)


def sweep_kernel(
    dims,
    x_ref,
    mf_ref,
    mb_ref,
    wj_ref,
    wc_ref,
    out_ref,
    mine,
    theirs,
    table_v,
    table_s,
    cand,
    packed,
    landed,
    aligned,
    h_ref,
    z_ref,
    edge_out,
    edge_in,
    m_send,
    m_recv,
    f_send,
    f_recv,
    e_send,
    e_recv,
    t_sem,
):
    frame_count, rows, cols, channels, layers, devices = dims
    lanes = 2 * channels
    bcols = cols // BS
    bc = rows // BS * bcols
    cap = bc // (2 * REACH)
    cell = BS * BS
    own = rows * cols
    halo = layers * cols
    me = lax.axis_index("tiles")

    def present(offset):
        return (me + offset >= 0) & (me + offset < devices)

    def motion_copy(oi):
        return pltpu.make_async_remote_copy(
            src_ref=mine,
            dst_ref=theirs.at[len(OFFSETS) - 1 - oi],
            send_sem=m_send.at[oi],
            recv_sem=m_recv.at[len(OFFSETS) - 1 - oi],
            device_id={"tiles": me + OFFSETS[oi]},
            device_id_type=pl.DeviceIdType.MESH,
        )

    def motion_arrival(oi):
        return pltpu.make_async_remote_copy(
            src_ref=mine,
            dst_ref=theirs.at[oi],
            send_sem=m_send.at[oi],
            recv_sem=m_recv.at[oi],
            device_id={"tiles": me + OFFSETS[oi]},
            device_id_type=pl.DeviceIdType.MESH,
        )

    def feature_copy(step, oi, slot):
        return pltpu.make_async_remote_copy(
            src_ref=packed.at[step, oi],
            dst_ref=landed.at[step, slot],
            send_sem=f_send.at[step, oi],
            recv_sem=f_recv.at[step, slot],
            device_id={"tiles": me + OFFSETS[oi]},
            device_id_type=pl.DeviceIdType.MESH,
        )

    def edge_copy(step, side, slot):
        return pltpu.make_async_remote_copy(
            src_ref=edge_out.at[step, side],
            dst_ref=edge_in.at[step, slot],
            send_sem=e_send.at[step, side],
            recv_sem=e_recv.at[step, slot],
            device_id={"tiles": me + (1 if side else -1)},
            device_id_type=pl.DeviceIdType.MESH,
        )

    barrier = pltpu.get_barrier_semaphore()
    for offset in OFFSETS:
        @pl.when(present(offset))
        def _():
            pl.semaphore_signal(
                barrier, inc=1, device_id={"tiles": me + offset},
                device_id_type=pl.DeviceIdType.MESH,
            )

    mine[...] = jnp.zeros(mine.shape, jnp.int32)
    for step in range(frame_count - 1):
        mine[step:step + 1, 0:bc] = mf_ref[step:step + 1, :]
        back = frame_count - 2 - step
        mine[frame_count - 1 + step:frame_count + step, 0:bc] = mb_ref[back:back + 1, :]

    peers = jnp.minimum(me, REACH) + jnp.minimum(devices - 1 - me, REACH)
    pl.semaphore_wait(barrier, peers)

    for oi, offset in enumerate(OFFSETS):
        @pl.when(present(offset))
        def _():
            motion_copy(oi).start()

    lane = lax.broadcasted_iota(jnp.int32, mine.shape, 1)

    def prefix(flags):
        total = flags
        shift = 1
        while shift < bc:
            total = total + jnp.where(lane >= shift, pltpu.roll(total, shift, axis=1), 0)
            shift *= 2
        return total - flags

    def owned(motion, device):
        low = device * bc
        return (motion >= low) & (motion < low + bc) & (lane < bc)

    def build_tables():
        motion = mine[...]
        picks = jnp.where(owned(motion, me), motion - me * bc, 0)
        for oi, offset in enumerate(OFFSETS):
            match = owned(motion, me + offset)
            rank = prefix(match.astype(jnp.int32))
            picks = picks + jnp.where(match, bc + cap * oi + jnp.minimum(rank, cap - 1), 0)
        table_v[len(OFFSETS)] = picks
        for oi, offset in enumerate(OFFSETS):
            @pl.when(present(offset))
            def _():
                motion_copy(oi).wait_send()
                motion_arrival(oi).wait_recv()
                wanted = theirs[oi]
                match = owned(wanted, me)
                rank = prefix(match.astype(jnp.int32))
                gathered = jnp.zeros(mine.shape, jnp.int32)
                for slot in range(cap):
                    value = jnp.where(match & (rank == slot), wanted - me * bc, 0)
                    shift = 1
                    while shift < bc:
                        value = value + pltpu.roll(value, shift, axis=1)
                        shift *= 2
                    value = pltpu.roll(value, 1 + slot, axis=1)
                    gathered = jnp.where(lane == bc + slot, value, gathered)
                table_v[oi] = gathered

            @pl.when(jnp.logical_not(present(offset)))
            def _():
                table_v[oi] = jnp.zeros(mine.shape, jnp.int32)
        load = pltpu.make_async_copy(table_v, table_s, t_sem)
        load.start()
        load.wait()

    half = lax.broadcasted_iota(jnp.int32, (rows, BS, lanes), 2) < channels

    def frame_step(t, carry):
        @pl.when(t == 0)
        def _():
            aligned[...] = jnp.zeros(aligned.shape, aligned.dtype)

        @pl.when(t > 0)
        def _():
            step = t - 1
            for oi, offset in enumerate(OFFSETS):
                @pl.when(present(offset))
                def _():
                    for slot in range(cap):
                        ahead = table_s[oi, step, bc + slot]
                        behind = table_s[oi, frame_count - 1 + step, bc + slot]
                        block = jnp.where(half, cand[ahead], cand[behind])
                        packed[step, oi, slot * cell:(slot + 1) * cell, :] = block.reshape(
                            cell, lanes
                        ).astype(jnp.bfloat16)
                    feature_copy(step, oi, len(OFFSETS) - 1 - oi).start()
            for oi, offset in enumerate(OFFSETS):
                @pl.when(present(offset))
                def _():
                    feature_copy(step, oi, oi).wait_recv()
                    cand[bc + cap * oi:bc + cap * (oi + 1)] = (
                        landed[step, oi].astype(jnp.float32).reshape(cap, BS, BS, lanes)
                    )
            for j in range(bc):
                ahead = table_s[len(OFFSETS), step, j]
                behind = table_s[len(OFFSETS), frame_count - 1 + step, j]
                aligned[:, j * BS:(j + 1) * BS, :] = jnp.where(half, cand[ahead], cand[behind])

        both = jnp.concatenate(
            [aligned[...].reshape(own, lanes).astype(jnp.bfloat16), x_ref[t]], axis=1
        )
        first = jnp.dot(both, wj_ref[...], preferred_element_type=jnp.float32).astype(jnp.bfloat16)
        h_ref[halo:halo + own, :] = first
        edge_out[t, 0] = first[:halo]
        edge_out[t, 1] = first[own - halo:]
        for side in range(2):
            @pl.when(present(1 if side else -1))
            def _():
                edge_copy(t, side, 1 - side).start()
        z_ref[0, halo:halo + own, :] = leaky(first.astype(jnp.float32)).astype(jnp.bfloat16)

        @pl.when(t == 0)
        def _():
            build_tables()

        for side in range(2):
            start = side * (halo + own)

            @pl.when(present(1 if side else -1))
            def _():
                edge_copy(t, side, side).wait_recv()
                edge = edge_in[t, side]
                h_ref[start:start + halo, :] = edge
                z_ref[0, start:start + halo, :] = leaky(edge.astype(jnp.float32)).astype(jnp.bfloat16)

            @pl.when(jnp.logical_not(present(1 if side else -1)))
            def _():
                h_ref[start:start + halo, :] = jnp.zeros((halo, lanes), jnp.bfloat16)
                z_ref[0, start:start + halo, :] = jnp.zeros((halo, lanes), jnp.bfloat16)

        for layer in range(layers):
            out_rows = rows + 2 * (layers - 1 - layer)
            size = out_rows * cols
            source = z_ref.at[layer % 2]
            target = z_ref.at[1 - layer % 2]
            stack = jnp.concatenate(
                [source[(layer + k) * cols:(layer + k) * cols + size, :] for k in range(3)], axis=1
            )
            summed = jnp.dot(stack, wc_ref[layer], preferred_element_type=jnp.float32)
            place = lax.broadcasted_iota(jnp.int32, (size, lanes), 0) % cols
            left = pltpu.roll(summed[:, :lanes], 1, axis=0)
            right = pltpu.roll(summed[:, 2 * lanes:], size - 1, axis=0)
            base = (layer + 1) * cols
            total = h_ref[base:base + size, :].astype(jnp.float32) + summed[:, lanes:2 * lanes]
            total = total + jnp.where(place == 0, 0.0, left)
            total = total + jnp.where(place == cols - 1, 0.0, right)
            rounded = total.astype(jnp.bfloat16)
            if layer < layers - 1:
                h_ref[base:base + size, :] = rounded
                target[base:base + size, :] = leaky(rounded.astype(jnp.float32)).astype(jnp.bfloat16)
                outside = halo - base

                @pl.when(me == 0)
                def _():
                    target[base:halo, :] = jnp.zeros((outside, lanes), jnp.bfloat16)

                @pl.when(me == devices - 1)
                def _():
                    target[halo + own:halo + own + outside, :] = jnp.zeros(
                        (outside, lanes), jnp.bfloat16
                    )
            else:
                out_ref[t] = rounded
                grid = rounded.astype(jnp.float32).reshape(rows, bcols, BS, lanes)
                for j in range(bcols):
                    cand[j] = grid[:, j]
        return carry

    lax.fori_loop(0, frame_count, frame_step, 0)

    for step in range(frame_count):
        for side in range(2):
            @pl.when(present(1 if side else -1))
            def _():
                edge_copy(step, side, side).wait_send()
        if step < frame_count - 1:
            for oi, offset in enumerate(OFFSETS):
                @pl.when(present(offset))
                def _():
                    feature_copy(step, oi, oi).wait_send()


def on_device(frames, motion_forward, motion_backward, join_weight, conv_weight):
    frame_count, channels, rows, cols = frames.shape
    layers = conv_weight.shape[1]
    devices = lax.axis_size("tiles")
    lanes = 2 * channels
    own = rows * cols
    halo = layers * cols
    bc = rows // BS * (cols // BS)
    cap = bc // (2 * REACH)
    sides = len(OFFSETS)
    steps = frame_count - 1

    moved = frames.transpose(0, 2, 3, 1).reshape(frame_count, own, channels)
    x = jnp.concatenate([moved, moved[::-1]], axis=2)
    same = jnp.eye(2, dtype=jnp.bfloat16)
    joined = join_weight.reshape(2, channels, 2, channels).transpose(2, 0, 3, 1)
    wj = (joined[:, :, :, None, :] * same[None, :, None, :, None]).reshape(2 * lanes, lanes)
    taps = conv_weight.reshape(2, layers, 3, 3, channels, channels).transpose(1, 2, 0, 5, 3, 4)
    wc = (taps[:, :, :, :, :, None, :] * same[None, None, :, None, None, :, None]).reshape(
        layers, 3 * lanes, 3 * lanes
    )

    dims = (frame_count, rows, cols, channels, layers, devices)
    vmem = pl.BlockSpec(memory_space=pltpu.VMEM)
    out = pl.pallas_call(
        functools.partial(sweep_kernel, dims),
        out_shape=jax.ShapeDtypeStruct((frame_count, own, lanes), jnp.bfloat16),
        in_specs=[vmem] * 5,
        out_specs=vmem,
        scratch_shapes=[
            pltpu.VMEM((8, 128), jnp.int32),
            pltpu.VMEM((sides, 8, 128), jnp.int32),
            pltpu.VMEM((sides + 1, 8, 128), jnp.int32),
            pltpu.SMEM((sides + 1, 8, 128), jnp.int32),
            pltpu.VMEM((bc + sides * cap, BS, BS, lanes), jnp.float32),
            pltpu.VMEM((steps, sides, cap * BS * BS, lanes), jnp.bfloat16),
            pltpu.VMEM((steps, sides, cap * BS * BS, lanes), jnp.bfloat16),
            pltpu.VMEM((rows, cols, lanes), jnp.float32),
            pltpu.VMEM((own + 2 * halo, lanes), jnp.bfloat16),
            pltpu.VMEM((2, own + 2 * halo, lanes), jnp.bfloat16),
            pltpu.VMEM((frame_count, 2, halo, lanes), jnp.bfloat16),
            pltpu.VMEM((frame_count, 2, halo, lanes), jnp.bfloat16),
            pltpu.SemaphoreType.DMA((sides,)),
            pltpu.SemaphoreType.DMA((sides,)),
            pltpu.SemaphoreType.DMA((steps, sides)),
            pltpu.SemaphoreType.DMA((steps, sides)),
            pltpu.SemaphoreType.DMA((frame_count, 2)),
            pltpu.SemaphoreType.DMA((frame_count, 2)),
            pltpu.SemaphoreType.DMA,
        ],
        compiler_params=pltpu.CompilerParams(
            collective_id=0, has_side_effects=True, vmem_limit_bytes=56 * 1024 * 1024
        ),
    )(x, motion_forward, motion_backward, wj, wc)
    out = out.reshape(frame_count, rows, cols, 2, channels)
    forward = out[:, :, :, 0].transpose(0, 3, 1, 2)
    backward = out[::-1, :, :, 1].transpose(0, 3, 1, 2)
    return forward, backward


def solution(mesh):
    return jax.shard_map(
        on_device,
        mesh=mesh,
        in_specs=(
            P(None, None, ("clips", "tiles"), None),
            P(None, ("clips", "tiles")),
            P(None, ("clips", "tiles")),
            P(),
            P(),
        ),
        out_specs=(
            P(None, None, ("clips", "tiles"), None),
            P(None, None, ("clips", "tiles"), None),
        ),
        check_vma=False,
    )
```

profile of v0, /device:TPU:11, one launch (start us, length us, event | category | flops | bytes accessed | tf_op | source)
XLA Modules:
  0.0 73.1 jit_solution(7430898481619078945)
XLA Ops:
  0.6 1.5 %copy.12 = bf16[4,8,128,64]{3,2,1,0:T(8,128)(2,1)S(1)} copy(bf16[4,8,128,64]{2,1,3,0:T(8,128)(2,1)} %bitcast.25) | data formatting | bytes 1048576 | tf_op jit(solution)/shard_map/transpose | solution.py:300
  2.1 0.1 rev.6
  2.2 0.0 copy-start.1
  2.2 0.0 copy-start
  2.2 1.5 %pad_maximum_fusion.x_ref = bf16[4,1024,128]{2,1,0:T(8,128)(2,1)} fusion(bf16[4,1024,64]{2,1,0:T(8,128)(2,1)S(1)} %rev.6, bf16[4,1024,64]{2,1,0:T(8,128)(2,1)S(1)} %bitcast.21), kind=kLoop, calls=%fused_computation | loop fusion | flops 2097152 | bytes 2097152 | tf_op jit(solution)/shard_map/concatenate | solution.py:301
  3.8 0.0 copy-done.1
  3.8 0.1 reshape.42
  3.9 0.1 copy.13
  4.0 0.2 broadcast_multiply_fusion.1
  4.2 0.7 %mul.40.wj_ref = bf16[256,128]{1,0:T(8,128)(2,1)} reshape(bf16[2,2,64,2,64]{4,3,2,1,0:T(2,128)(2,1)S(1)} %broadcast_multiply_fusion.1) | data formatting | bytes 131072 | tf_op jit(solution)/shard_map/mul | solution.py:304
  4.9 0.0 copy-done
  4.9 2.3 %copy.14 = bf16[4,3,2,64,3,64]{5,4,3,2,1,0:T(4,128)(2,1)} copy(bf16[4,3,2,64,3,64]{3,5,4,1,0,2:T(8,128)(2,1)S(1)} %bitcast.24) | data formatting | bytes 1179648 | tf_op jit(solution)/shard_map/transpose | solution.py:305
  7.2 3.5 %mul.41 = bf16[4,3,2,64,3,2,64]{6,5,4,3,2,1,0:T(2,128)(2,1)S(1)} broadcast(bf16[4,3,2,64,3,64]{5,4,3,2,1,0:T(4,128)(2,1)} %copy.14), dimensions={0,1,2,3,4,6} | broadcast | bytes 1769472 | tf_op jit(solution)/shard_map/mul | solution.py:306
  10.7 1.5 %mul.42 = bf16[4,384,384]{2,1,0:T(8,128)(2,1)S(1)} reshape(bf16[4,3,2,64,3,2,64]{6,5,4,3,2,1,0:T(2,128)(2,1)S(1)} %mul.41) | data formatting | bytes 2359296 | tf_op jit(solution)/shard_map/mul | solution.py:306
  12.2 0.4 mul.43
  12.6 0.4 mul.44
  13.0 1.2 %broadcast_multiply_fusion.wc_ref = bf16[4,384,384]{2,1,0:T(8,128)(2,1)} fusion(bf16[4,384,384]{2,1,0:T(8,128)(2,1)S(1)} %mul.42, bf16[384,384]{1,0:T(8,128)(2,1)S(1)} %mul.44), kind=kLoop, calls=%fused_computation.1 | loop fusion | flops 589824 | bytes 2654208 | tf_op jit(solution)/shard_map/mul | solution.py:306
  14.2 55.5 %shard_map.68 = bf16[4,1024,128]{2,1,0:T(8,128)(2,1)} custom-call(bf16[4,1024,128]{2,1,0:T(8,128)(2,1)} %pad_maximum_fusion.x_ref, s32[3,16]{1,0:T(4,128)} %mf_ref.1, s32[3,16]{1,0:T(4,128)} %mb_ref.1, bf16[256,128]{1,0:T(8,128)(2,1)} %mul.40.wj_ref, bf16[4,384,384]{2,1,0:T(8,128)(2,1)} %broadcast_multiply_fusion.wc_ref), custom_call_target="tpu_custom_call" | custom-call | tf_op jit(solution)/shard_map/pallas_call | solution.py:312
  69.6 1.5 %copy.15 = bf16[4,1024,128]{1,2,0:T(8,128)(2,1)S(1)} copy(bf16[4,1024,128]{2,1,0:T(8,128)(2,1)} %shard_map.68) | data formatting | bytes 2097152 | tf_op jit(solution)/shard_map/pallas_call | solution.py:312
  71.1 0.3 copy.16
  71.4 0.9 %fusion = (bf16[4,8,128,1,64]{2,1,4,3,0:T(8,128)(2,1)S(1)}, bf16[4,64,8,128]{3,2,1,0:T(8,128)(2,1)}) fusion(bf16[4,8,128,2,64]{2,1,4,3,0:T(8,128)(2,1)S(1)} %bitcast.22), kind=kLoop, calls=%fused_computation.6 | loop fusion | bytes 2097152 | tf_op jit(solution)/shard_map/slice | solution.py:344
  72.3 0.8 %reverse_bitcast_fusion = bf16[4,64,8,128]{3,2,1,0:T(8,128)(2,1)} fusion(bf16[4,8,128,1,64]{2,1,4,3,0:T(8,128)(2,1)S(1)} %get-tuple-element.2), kind=kLoop, calls=%fused_computation.3 | loop fusion | bytes 1048576 | tf_op jit(solution)/shard_map/transpose | solution.py:344
  (1 shorter events, 0.0 us)
Async XLA Ops:
  2.2 1.6 %copy-start.1 = (bf16[2,64,128]{2,1,0:T(8,128)(2,1)S(1)}, bf16[2,64,128]{2,1,0:T(8,128)(2,1)}, u32[]{:S(2)}) copy-start(bf16[2,64,128]{2,1,0:T(8,128)(2,1)} %param.8) | copy-start | bytes 98308
  2.2 2.7 %copy-start = (bf16[2,4,9,64,64]{4,3,2,1,0:T(8,128)(2,1)S(1)}, bf16[2,4,9,64,64]{4,3,2,1,0:T(8,128)(2,1)}, u32[]{:S(2)}) copy-start(bf16[2,4,9,64,64]{4,3,2,1,0:T(8,128)(2,1)} %param.9) | copy-start | bytes 1769476
where the time goes:
time: 73.6 us; the launch traced here: 73.1 us
  Pallas kernels  55.5 us (75%)
  local copies, waits for them, and re-layouts  14 us (19%)
  other arithmetic  2.92 us (4%)
    pallas_call x1, Pallas kernels, on_device(): pl.pallas_call(functools.partial(sweep_kernel, dims), out_shape=jax.Shape...  55.5 us
    mul x4, local copies, waits for them, and re-layouts, on_device(): taps[:, :, :, :, :, None, :] * same[None, None, :, None, None, :, None]  5.7 us
    transpose x1, local copies, waits for them, and re-layouts, on_device(): conv_weight.reshape(2, layers, 3, 3, channels, channels)  2.3 us
    concatenate x1, other arithmetic, on_device(): x = jnp.concatenate([moved, moved[::-1]], axis=2)  1.55 us
    transpose x1, local copies, waits for them, and re-layouts, on_device(): moved = frames.transpose(0, 2, 3, 1).reshape(frame_count, own, channels)  1.51 us
    pallas_call x1, local copies, waits for them, and re-layouts, on_device(): pl.pallas_call(functools.partial(sweep_kernel, dims), out_shape=jax.Shape...  1.49 us

commit v1 on v0

v1 whole, which is shorter than its diff:
```python
import functools

import jax
import jax.numpy as jnp
from jax import lax
from jax.experimental import pallas as pl
from jax.experimental.pallas import tpu as pltpu
from jax.sharding import PartitionSpec as P

BS = 8
REACH = 2
OFFSETS = tuple(o for o in range(-REACH, REACH + 1) if o != 0)


def leaky(value):
    return jnp.where(value >= 0, value, 0.1 * value)


def blockdiag(tile):
    blank = jnp.zeros(tile.shape, tile.dtype)
    return jnp.concatenate(
        [jnp.concatenate([tile, blank], axis=1), jnp.concatenate([blank, tile], axis=1)], axis=0
    )


def matmul_t(left, right):
    return lax.dot_general(
        left, right, (((1,), (1,)), ((), ())), preferred_element_type=jnp.float32
    )


def sweep_kernel(
    dims,
    x_ref,
    mf_ref,
    mb_ref,
    join_ref,
    conv_ref,
    ahead_ref,
    behind_ref,
    wj_ref,
    wc_ref,
    mine,
    theirs,
    table_v,
    table_s,
    cand,
    packed,
    landed,
    aligned,
    h_ref,
    z_ref,
    edge_out,
    edge_in,
    m_send,
    m_recv,
    f_send,
    f_recv,
    e_send,
    e_recv,
    t_sem,
):
    frame_count, rows, cols, channels, layers, devices = dims
    outs = (ahead_ref, behind_ref)
    lanes = 2 * channels
    width = cols // 2
    bc = cols // BS
    pairs = bc // 2
    cap = bc // (2 * REACH)
    sides = len(OFFSETS)
    kept = pairs + sides * cap // 2
    cell = BS * BS
    own = rows * width
    halo = layers * width
    me = lax.axis_index("tiles")

    def present(offset):
        return (me + offset >= 0) & (me + offset < devices)

    def remote(source, target, send, receive, offset):
        return pltpu.make_async_remote_copy(
            src_ref=source,
            dst_ref=target,
            send_sem=send,
            recv_sem=receive,
            device_id={"tiles": me + offset},
            device_id_type=pl.DeviceIdType.MESH,
        )

    def motion_copy(oi, slot):
        return remote(mine, theirs.at[slot], m_send.at[oi], m_recv.at[slot], OFFSETS[oi])

    def feature_copy(d, step, oi, slot):
        return remote(
            packed.at[d, step, oi], landed.at[d, step, slot],
            f_send.at[d, step, oi], f_recv.at[d, step, slot], OFFSETS[oi],
        )

    def edge_copy(d, step, side, slot):
        return remote(
            edge_out.at[d, step, side], edge_in.at[d, step, slot],
            e_send.at[d, step, side], e_recv.at[d, step, slot], 1 if side else -1,
        )

    barrier = pltpu.get_barrier_semaphore()
    for offset in OFFSETS:
        @pl.when(present(offset))
        def _():
            pl.semaphore_signal(
                barrier, inc=1, device_id={"tiles": me + offset},
                device_id_type=pl.DeviceIdType.MESH,
            )

    mine[...] = jnp.zeros(mine.shape, jnp.int32)
    for step in range(frame_count - 1):
        mine[step:step + 1, 0:bc] = mf_ref[step:step + 1, :]
        back = frame_count - 2 - step
        mine[frame_count - 1 + step:frame_count + step, 0:bc] = mb_ref[back:back + 1, :]

    for d in range(2):
        joined = join_ref[d]
        wj_ref[d, :, :lanes] = blockdiag(joined[:, :channels])
        wj_ref[d, :, lanes:] = blockdiag(joined[:, channels:])

        def build_layer(layer, carry):
            for tap in range(9):
                down, across = tap // 3, tap % 3
                wc_ref[
                    d, layer, across * lanes:(across + 1) * lanes, down * lanes:(down + 1) * lanes
                ] = blockdiag(conv_ref[d, layer, tap])
            return carry

        lax.fori_loop(0, layers, build_layer, 0)

    peers = jnp.minimum(me, REACH) + jnp.minimum(devices - 1 - me, REACH)
    pl.semaphore_wait(barrier, peers)

    for oi, offset in enumerate(OFFSETS):
        @pl.when(present(offset))
        def _():
            motion_copy(oi, sides - 1 - oi).start()

    lane = lax.broadcasted_iota(jnp.int32, mine.shape, 1)

    def prefix(flags):
        total = flags
        shift = 1
        while shift < bc:
            total = total + jnp.where(lane >= shift, pltpu.roll(total, shift, axis=1), 0)
            shift *= 2
        return total - flags

    def owned(motion, device):
        low = device * bc
        return (motion >= low) & (motion < low + bc) & (lane < bc)

    def own_code(local):
        return jnp.where(local < pairs, local, kept + local - pairs)

    def swapped(code):
        return jnp.where(code >= kept, code - kept, code + kept)

    def build_tables():
        motion = mine[...]
        picks = jnp.where(owned(motion, me), own_code(motion - me * bc), 0)
        for oi, offset in enumerate(OFFSETS):
            match = owned(motion, me + offset)
            rank = jnp.minimum(prefix(match.astype(jnp.int32)), cap - 1)
            base = pairs + oi * cap // 2
            code = jnp.where(rank < cap // 2, base + rank, kept + base + rank - cap // 2)
            picks = picks + jnp.where(match, code, 0)
        table_v[sides] = jnp.where(lane < pairs, picks, swapped(picks))
        for oi, offset in enumerate(OFFSETS):
            @pl.when(present(offset))
            def _():
                motion_copy(oi, oi).wait_send()
                motion_copy(oi, oi).wait_recv()
                wanted = theirs[oi]
                match = owned(wanted, me)
                rank = prefix(match.astype(jnp.int32))
                code = own_code(wanted - me * bc)
                gathered = jnp.zeros(mine.shape, jnp.int32)
                for slot in range(cap):
                    held = code if slot < cap // 2 else swapped(code)
                    value = jnp.where(match & (rank == slot), held, 0)
                    shift = 1
                    while shift < bc:
                        value = value + pltpu.roll(value, shift, axis=1)
                        shift *= 2
                    value = pltpu.roll(value, 1 + slot, axis=1)
                    gathered = jnp.where(lane == bc + slot, value, gathered)
                table_v[oi] = gathered

            @pl.when(jnp.logical_not(present(offset)))
            def _():
                table_v[oi] = jnp.zeros(mine.shape, jnp.int32)
        load = pltpu.make_async_copy(table_v, table_s, t_sem)
        load.start()
        load.wait()

    left_half = lax.broadcasted_iota(jnp.int32, (rows, BS, lanes), 2) < channels

    def keep(d, index, tile):
        cand[d, index] = tile
        cand[d, kept + index] = pltpu.roll(tile, channels, axis=2)

    def begin(d, t):
        @pl.when(t == 0)
        def _():
            aligned[d] = jnp.zeros(aligned.shape[1:], aligned.dtype)

        @pl.when(t > 0)
        def _():
            step = t - 1
            row = d * (frame_count - 1) + step
            for oi, offset in enumerate(OFFSETS):
                @pl.when(present(offset))
                def _():
                    feature_copy(d, step, oi, oi).wait_recv()
                    tiles = landed[d, step, oi].astype(jnp.float32)
                    tiles = tiles.reshape(cap // 2, BS, BS, lanes)
                    for pair in range(cap // 2):
                        keep(d, pairs + oi * cap // 2 + pair, tiles[pair])
            for j in range(pairs):
                low = table_s[sides, row, j]
                high = table_s[sides, row, pairs + j]
                aligned[d, :, j * BS:(j + 1) * BS, :] = jnp.where(
                    left_half, cand[d, low], cand[d, high]
                )

        now = t if d == 0 else frame_count - 1 - t
        both = jnp.concatenate(
            [aligned[d].reshape(own, lanes).astype(jnp.bfloat16), x_ref[now]], axis=1
        )
        first = matmul_t(both, wj_ref[d]).astype(jnp.bfloat16)
        edge_out[d, t, 0] = first[:halo]
        edge_out[d, t, 1] = first[own - halo:]
        for side in range(2):
            @pl.when(present(1 if side else -1))
            def _():
                edge_copy(d, t, side, 1 - side).start()
        h_ref[d, halo:halo + own, :] = first
        z_ref[d, 0, halo:halo + own, :] = leaky(first.astype(jnp.float32)).astype(jnp.bfloat16)

    def finish(d, t):
        for side in range(2):
            start = side * (halo + own)

            @pl.when(present(1 if side else -1))
            def _():
                edge_copy(d, t, side, side).wait_recv()
                edge = edge_in[d, t, side]
                h_ref[d, start:start + halo, :] = edge
                z_ref[d, 0, start:start + halo, :] = leaky(edge.astype(jnp.float32)).astype(
                    jnp.bfloat16
                )

            @pl.when(jnp.logical_not(present(1 if side else -1)))
            def _():
                h_ref[d, start:start + halo, :] = jnp.zeros((halo, lanes), jnp.bfloat16)
                z_ref[d, 0, start:start + halo, :] = jnp.zeros((halo, lanes), jnp.bfloat16)

        for layer in range(layers):
            out_rows = rows + 2 * (layers - 1 - layer)
            size = out_rows * width
            source = z_ref.at[d, layer % 2]
            target = z_ref.at[d, 1 - layer % 2]
            stack = jnp.concatenate(
                [source[(layer + k) * width:(layer + k) * width + size, :] for k in range(3)],
                axis=1,
            )
            summed = matmul_t(stack, wc_ref[d, layer])
            place = lax.broadcasted_iota(jnp.int32, (out_rows, BS, lanes), 1)
            lefts = lax.broadcasted_iota(jnp.int32, (out_rows, BS, lanes), 2) < channels
            before = pltpu.roll(summed[:, :lanes].reshape(out_rows, width, lanes), 1, axis=1)
            seam = before[:, :BS]
            crossed = jnp.where(lefts, 0.0, pltpu.roll(seam, channels, axis=2))
            before = jnp.concatenate(
                [jnp.where(place == 0, crossed, seam), before[:, BS:]], axis=1
            ).reshape(size, lanes)
            after = pltpu.roll(
                summed[:, 2 * lanes:].reshape(out_rows, width, lanes), width - 1, axis=1
            )
            seam = after[:, width - BS:]
            crossed = jnp.where(lefts, pltpu.roll(seam, channels, axis=2), 0.0)
            after = jnp.concatenate(
                [after[:, :width - BS], jnp.where(place == BS - 1, crossed, seam)], axis=1
            ).reshape(size, lanes)
            base = (layer + 1) * width
            total = h_ref[d, base:base + size, :].astype(jnp.float32) + summed[:, lanes:2 * lanes]
            rounded = (total + before + after).astype(jnp.bfloat16)
            if layer < layers - 1:
                h_ref[d, base:base + size, :] = rounded
                target[base:base + size, :] = leaky(rounded.astype(jnp.float32)).astype(jnp.bfloat16)
                outside = halo - base

                @pl.when(me == 0)
                def _():
                    target[base:halo, :] = jnp.zeros((outside, lanes), jnp.bfloat16)

                @pl.when(me == devices - 1)
                def _():
                    target[halo + own:halo + own + outside, :] = jnp.zeros(
                        (outside, lanes), jnp.bfloat16
                    )
            else:
                grid = rounded.astype(jnp.float32).reshape(rows, pairs, BS, lanes)
                for j in range(pairs):
                    keep(d, j, grid[:, j])
                now = t if d == 0 else frame_count - 1 - t
                outs[d][now] = rounded

        @pl.when(t < frame_count - 1)
        def _():
            row = d * (frame_count - 1) + t
            for oi, offset in enumerate(OFFSETS):
                @pl.when(present(offset))
                def _():
                    for pair in range(cap // 2):
                        low = table_s[oi, row, bc + pair]
                        high = table_s[oi, row, bc + cap // 2 + pair]
                        block = jnp.where(left_half, cand[d, low], cand[d, high])
                        packed[d, t, oi, pair * cell:(pair + 1) * cell, :] = block.reshape(
                            cell, lanes
                        ).astype(jnp.bfloat16)
                    feature_copy(d, t, oi, sides - 1 - oi).start()

    def frame_step(t, carry):
        begin(0, t)
        begin(1, t)

        @pl.when(t == 0)
        def _():
            build_tables()

        finish(0, t)
        finish(1, t)
        return carry

    lax.fori_loop(0, frame_count, frame_step, 0)

    for d in range(2):
        for step in range(frame_count):
            for side in range(2):
                @pl.when(present(1 if side else -1))
                def _():
                    edge_copy(d, step, side, side).wait_send()
            if step < frame_count - 1:
                for oi, offset in enumerate(OFFSETS):
                    @pl.when(present(offset))
                    def _():
                        feature_copy(d, step, oi, oi).wait_send()


def on_device(frames, motion_forward, motion_backward, join_weight, conv_weight):
    frame_count, channels, rows, cols = frames.shape
    layers = conv_weight.shape[1]
    devices = lax.axis_size("tiles")
    lanes = 2 * channels
    width = cols // 2
    own = rows * width
    halo = layers * width
    bc = rows // BS * (cols // BS)
    cap = bc // (2 * REACH)
    sides = len(OFFSETS)
    steps = frame_count - 1
    kept = bc // 2 + sides * cap // 2

    x = frames.reshape(frame_count, channels, rows, 2, width).transpose(0, 2, 4, 3, 1)
    x = x.reshape(frame_count, own, lanes)

    dims = (frame_count, rows, cols, channels, layers, devices)
    vmem = pl.BlockSpec(memory_space=pltpu.VMEM)
    result = jax.ShapeDtypeStruct((frame_count, own, lanes), jnp.bfloat16)
    outs = pl.pallas_call(
        functools.partial(sweep_kernel, dims),
        out_shape=(result, result),
        in_specs=[vmem] * 5,
        out_specs=(vmem, vmem),
        scratch_shapes=[
            pltpu.VMEM((2, lanes, 2 * lanes), jnp.bfloat16),
            pltpu.VMEM((2, layers, 3 * lanes, 3 * lanes), jnp.bfloat16),
            pltpu.VMEM((8, 128), jnp.int32),
            pltpu.VMEM((sides, 8, 128), jnp.int32),
            pltpu.VMEM((sides + 1, 8, 128), jnp.int32),
            pltpu.SMEM((sides + 1, 8, 128), jnp.int32),
            pltpu.VMEM((2, 2 * kept, BS, BS, lanes), jnp.float32),
            pltpu.VMEM((2, steps, sides, cap // 2 * BS * BS, lanes), jnp.bfloat16),
            pltpu.VMEM((2, steps, sides, cap // 2 * BS * BS, lanes), jnp.bfloat16),
            pltpu.VMEM((2, rows, width, lanes), jnp.float32),
            pltpu.VMEM((2, own + 2 * halo, lanes), jnp.bfloat16),
            pltpu.VMEM((2, 2, own + 2 * halo, lanes), jnp.bfloat16),
            pltpu.VMEM((2, frame_count, 2, halo, lanes), jnp.bfloat16),
            pltpu.VMEM((2, frame_count, 2, halo, lanes), jnp.bfloat16),
            pltpu.SemaphoreType.DMA((sides,)),
            pltpu.SemaphoreType.DMA((sides,)),
            pltpu.SemaphoreType.DMA((2, steps, sides)),
            pltpu.SemaphoreType.DMA((2, steps, sides)),
            pltpu.SemaphoreType.DMA((2, frame_count, 2)),
            pltpu.SemaphoreType.DMA((2, frame_count, 2)),
            pltpu.SemaphoreType.DMA,
        ],
        compiler_params=pltpu.CompilerParams(
            collective_id=0, has_side_effects=True, vmem_limit_bytes=56 * 1024 * 1024
        ),
    )(x, motion_forward, motion_backward, join_weight, conv_weight)

    def placed(out):
        out = out.reshape(frame_count, rows, width, 2, channels)
        return out.transpose(0, 4, 1, 3, 2).reshape(frame_count, channels, rows, cols)

    return placed(outs[0]), placed(outs[1])


def solution(mesh):
    return jax.shard_map(
        on_device,
        mesh=mesh,
        in_specs=(
            P(None, None, ("clips", "tiles"), None),
            P(None, ("clips", "tiles")),
            P(None, ("clips", "tiles")),
            P(),
            P(),
        ),
        out_specs=(
            P(None, None, ("clips", "tiles"), None),
            P(None, None, ("clips", "tiles"), None),
        ),
        check_vma=False,
    )
```

time: 73.6 us -> 65.6 us (0.89)
  Pallas kernels: 55.5 us -> 48.8 us
  other arithmetic: 2.92 us -> 0 us
  local copies, waits for them, and re-layouts: 14 us -> 15.9 us
    reshape x1 -> x7, local copies, waits for them, and re-layouts: 0.09 us -> 11.4 us  [the longest x2 4.72 us: on_device(): frames.reshape(frame_count, channels, rows, 2, width)]
    pallas_call x1, Pallas kernels: 55.5 us -> 48.8 us  [on_device(): pl.pallas_call(functools.partial(sweep_kernel, dims), out_shape=(result,...]
    mul x5 -> x0, local copies, waits for them, and re-layouts: 6.45 us -> none  [the longest x4 5.7 us: on_device(): taps[:, :, :, :, :, None, :] * same[None, None, :, None, None, :, None]]
    concatenate x1 -> x0, other arithmetic: 1.55 us -> none  [on_device(): x = jnp.concatenate([moved, moved[::-1]], axis=2)]
    pallas_call x1 -> x0, local copies, waits for them, and re-layouts: 1.49 us -> none  [on_device(): pl.pallas_call(functools.partial(sweep_kernel, dims), out_shape=jax.Shape...]
    mul x2 -> x0, other arithmetic: 1.36 us -> none  [the longest x1 1.19 us: on_device(): taps[:, :, :, :, :, None, :] * same[None, None, :, None, None, :, None]]
    slice x1 -> x0, local copies, waits for them, and re-layouts: 0.87 us -> none  [on_device(): backward = out[::-1, :, :, 1].transpose(0, 3, 1, 2)]
    transpose x4 -> x2, local copies, waits for them, and re-layouts: 4.74 us -> 4.47 us  [placed(): out.transpose(0, 4, 1, 3, 2).reshape(frame_count, channels, rows, cols)]
where the time goes in v1:
time: 65.6 us; the launch traced here: 65.4 us
  Pallas kernels  48.8 us (74%)
  local copies, waits for them, and re-layouts  15.9 us (24%)
  between operations  0.69 us (1%)
    pallas_call x1, Pallas kernels, on_device(): pl.pallas_call(functools.partial(sweep_kernel, dims), out_shape=(result,...  48.8 us
    reshape x2, local copies, waits for them, and re-layouts, on_device(): frames.reshape(frame_count, channels, rows, 2, width)  4.72 us
    transpose x2, local copies, waits for them, and re-layouts, placed(): out.transpose(0, 4, 1, 3, 2).reshape(frame_count, channels, rows, cols)  4.47 us
    reshape x2, local copies, waits for them, and re-layouts, placed(): out = out.reshape(frame_count, rows, width, 2, channels)  2.85 us
    reshape x2, local copies, waits for them, and re-layouts, placed(): out.transpose(0, 4, 1, 3, 2).reshape(frame_count, channels, rows, cols)  2.57 us

profile of v1, /device:TPU:11, one launch (start us, length us, event | category | flops | bytes accessed | tf_op | source)
XLA Modules:
  0.0 65.4 jit_solution(12134779826600861987)
XLA Ops:
  0.6 2.5 %reshape.22 = bf16[4,64,8,2,64]{4,3,2,1,0:T(2,128)(2,1)S(1)} reshape(bf16[4,64,8,128]{3,2,1,0:T(8,128)(2,1)} %param.5) | data formatting | bytes 1048576 | tf_op jit(solution)/shard_map/reshape | solution.py:369
  3.1 2.3 %copy.7 = bf16[4,64,8,2,64]{1,3,4,2,0:T(2,128)(2,1)S(1)} copy(bf16[4,64,8,2,64]{4,3,2,1,0:T(2,128)(2,1)S(1)} %reshape.22) | data formatting | bytes 1048576 | tf_op jit(solution)/shard_map/reshape | solution.py:369
  5.4 1.3 %reshape.23.x_ref = bf16[4,512,128]{2,1,0:T(8,128)(2,1)} reshape(bf16[4,8,64,2,64]{4,3,2,1,0:T(2,128)(2,1)S(1)} %bitcast.5) | data formatting | bytes 1048576 | tf_op jit(solution)/shard_map/reshape | solution.py:370
  6.6 48.8 %shard_map.68 = (bf16[4,512,128]{2,1,0:T(8,128)(2,1)}, bf16[4,512,128]{2,1,0:T(8,128)(2,1)}) custom-call(bf16[4,512,128]{2,1,0:T(8,128)(2,1)} %reshape.23.x_ref, s32[3,16]{1,0:T(4,128)} %mf_ref.1, s32[3,16]{1,0:T(4,128)} %mb_ref.1, bf16[2,64,128]{2,1,0:T(8,128)(2,1)} %join_ref.1, bf16[2,4,9,64,64]{4,3,2,1,0:T(8,128)(2,1)} %conv_ref.1), custom_call_target="tpu_custom_call" | custom-call | tf_op jit(solution)/shard_map/pallas_call | solution.py:375
  55.5 2.5 %reshape.24 = bf16[4,8,64,2,64]{4,3,2,1,0:T(2,128)(2,1)S(1)} reshape(bf16[4,512,128]{2,1,0:T(8,128)(2,1)} %get-tuple-element.4) | data formatting | bytes 1048576 | tf_op jit(solution)/shard_map/reshape | solution.py:409
  57.9 2.2 %copy.8 = bf16[4,64,8,2,64]{4,3,2,1,0:T(2,128)(2,1)S(1)} copy(bf16[4,64,8,2,64]{1,3,4,2,0:T(2,128)(2,1)S(1)} %bitcast.6) | data formatting | bytes 1048576 | tf_op jit(solution)/shard_map/transpose | solution.py:410
  60.2 0.0 copy-start
  60.2 1.3 %reshape.25 = bf16[4,64,8,128]{3,2,1,0:T(8,128)(2,1)} reshape(bf16[4,64,8,2,64]{4,3,2,1,0:T(2,128)(2,1)S(1)} %copy.8) | data formatting | bytes 1048576 | tf_op jit(solution)/shard_map/reshape | solution.py:410
  61.4 0.0 copy-done
  61.5 0.4 reshape.26
  61.9 2.2 %copy.9 = bf16[4,64,8,2,64]{4,3,2,1,0:T(2,128)(2,1)S(1)} copy(bf16[4,64,8,2,64]{1,3,4,2,0:T(2,128)(2,1)S(1)} %bitcast.7) | data formatting | bytes 1048576 | tf_op jit(solution)/shard_map/transpose | solution.py:410
  64.1 1.3 %reshape.27 = bf16[4,64,8,128]{3,2,1,0:T(8,128)(2,1)} reshape(bf16[4,64,8,2,64]{4,3,2,1,0:T(2,128)(2,1)S(1)} %copy.9) | data formatting | bytes 1048576 | tf_op jit(solution)/shard_map/reshape | solution.py:410
Async XLA Ops:
  60.2 1.3 %copy-start = (bf16[4,512,128]{2,1,0:T(8,128)(2,1)S(1)}, bf16[4,512,128]{2,1,0:T(8,128)(2,1)}, u32[]{:S(2)}) copy-start(bf16[4,512,128]{2,1,0:T(8,128)(2,1)} %get-tuple-element.5) | copy-start | bytes 1572868

commit v2 on v1

--- a/solution.py
+++ b/solution.py
@@ -31,13 +31,15 @@
 
 def sweep_kernel(
     dims,
-    x_ref,
+    frames_ref,
     mf_ref,
     mb_ref,
     join_ref,
     conv_ref,
     ahead_ref,
     behind_ref,
+    x_ref,
+    flip,
     wj_ref,
     wc_ref,
     mine,
@@ -132,6 +134,39 @@
 
         lax.fori_loop(0, layers, build_layer, 0)
 
+    def picker(count):
+        row = lax.broadcasted_iota(jnp.int32, (count, 2 * count), 0)
+        column = lax.broadcasted_iota(jnp.int32, (count, 2 * count), 1)
+        return ((column == row) | (column == row + count)).astype(jnp.bfloat16)
+
+    def load_frame(f, carry):
+        flip[0] = frames_ref[f].astype(jnp.float32).reshape(channels * rows, cols)
+        first = lax.broadcasted_iota(jnp.int32, (channels, cols), 1) < width
+        parts = []
+        for r in range(rows):
+            row = flip[0, pl.ds(r, channels, stride=rows), :]
+            parts += [jnp.where(first, row, 0.0), jnp.where(first, 0.0, row)]
+        moved = matmul_t(picker(width), jnp.concatenate(parts, axis=0).astype(jnp.bfloat16))
+        for r in range(rows):
+            x_ref[f, r * width:(r + 1) * width, :] = moved[:, r * lanes:(r + 1) * lanes].astype(
+                jnp.bfloat16
+            )
+        return carry
+
+    lax.fori_loop(0, frame_count, load_frame, 0)
+
+    def emit(d, t):
+        value = h_ref[d, halo:halo + own, :].astype(jnp.float32).reshape(rows, width, lanes)
+        first = lax.broadcasted_iota(jnp.int32, value.shape, 2) < channels
+        split = jnp.concatenate(
+            [jnp.where(first, value, 0.0), jnp.where(first, 0.0, value)], axis=1
+        ).reshape(rows * cols, lanes).astype(jnp.bfloat16)
+        moved = matmul_t(picker(channels), split)
+        for r in range(rows):
+            flip[d, pl.ds(r, channels, stride=rows), :] = moved[:, r * cols:(r + 1) * cols]
+        now = t if d == 0 else frame_count - 1 - t
+        outs[d][now] = flip[d].reshape(channels, rows, cols).astype(jnp.bfloat16)
+
     peers = jnp.minimum(me, REACH) + jnp.minimum(devices - 1 - me, REACH)
     pl.semaphore_wait(barrier, peers)
 
@@ -307,8 +342,7 @@
                 grid = rounded.astype(jnp.float32).reshape(rows, pairs, BS, lanes)
                 for j in range(pairs):
                     keep(d, j, grid[:, j])
-                now = t if d == 0 else frame_count - 1 - t
-                outs[d][now] = rounded
+                h_ref[d, base:base + size, :] = rounded
 
         @pl.when(t < frame_count - 1)
         def _():
@@ -335,6 +369,8 @@
 
         finish(0, t)
         finish(1, t)
+        emit(0, t)
+        emit(1, t)
         return carry
 
     lax.fori_loop(0, frame_count, frame_step, 0)
@@ -366,18 +402,17 @@
     steps = frame_count - 1
     kept = bc // 2 + sides * cap // 2
 
-    x = frames.reshape(frame_count, channels, rows, 2, width).transpose(0, 2, 4, 3, 1)
-    x = x.reshape(frame_count, own, lanes)
-
     dims = (frame_count, rows, cols, channels, layers, devices)
     vmem = pl.BlockSpec(memory_space=pltpu.VMEM)
-    result = jax.ShapeDtypeStruct((frame_count, own, lanes), jnp.bfloat16)
-    outs = pl.pallas_call(
+    result = jax.ShapeDtypeStruct(frames.shape, jnp.bfloat16)
+    return pl.pallas_call(
         functools.partial(sweep_kernel, dims),
         out_shape=(result, result),
         in_specs=[vmem] * 5,
         out_specs=(vmem, vmem),
         scratch_shapes=[
+            pltpu.VMEM((frame_count, own, lanes), jnp.bfloat16),
+            pltpu.VMEM((2, channels * rows, cols), jnp.float32),
             pltpu.VMEM((2, lanes, 2 * lanes), jnp.bfloat16),
             pltpu.VMEM((2, layers, 3 * lanes, 3 * lanes), jnp.bfloat16),
             pltpu.VMEM((8, 128), jnp.int32),
@@ -403,13 +438,7 @@
         compiler_params=pltpu.CompilerParams(
             collective_id=0, has_side_effects=True, vmem_limit_bytes=56 * 1024 * 1024
         ),
-    )(x, motion_forward, motion_backward, join_weight, conv_weight)
-
-    def placed(out):
-        out = out.reshape(frame_count, rows, width, 2, channels)
-        return out.transpose(0, 4, 1, 3, 2).reshape(frame_count, channels, rows, cols)
-
-    return placed(outs[0]), placed(outs[1])
+    )(frames, motion_forward, motion_backward, join_weight, conv_weight)
 
 
 def solution(mesh):

time: 65.6 us -> 53.3 us (0.81)
  local copies, waits for them, and re-layouts: 15.9 us -> 2.72 us
  Pallas kernels: 48.8 us -> 49.8 us
    reshape x7 -> x0, local copies, waits for them, and re-layouts: 11.4 us -> none  [the longest x2 4.72 us: on_device(): frames.reshape(frame_count, channels, rows, 2, width)]
    transpose x2 -> x0, local copies, waits for them, and re-layouts: 4.47 us -> none  [placed(): out.transpose(0, 4, 1, 3, 2).reshape(frame_count, channels, rows, cols)]
    unnamed x2 -> x4, local copies, waits for them, and re-layouts: 0.01 us -> 2.72 us
    pallas_call x1, Pallas kernels: 48.8 us -> 49.8 us  [on_device(): pl.pallas_call(functools.partial(sweep_kernel, dims), out_shape=(result,...]
where the time goes in v2:
time: 53.3 us; the launch traced here: 53.2 us
  Pallas kernels  49.8 us (93%)
  local copies, waits for them, and re-layouts  2.72 us (5%)
  between operations  0.65 us (1%)
    pallas_call x1, Pallas kernels, on_device(): pl.pallas_call(functools.partial(sweep_kernel, dims), out_shape=(result,...  49.8 us
    unnamed x4, local copies, waits for them, and re-layouts  2.72 us

profile of v2, /device:TPU:11, one launch (start us, length us, event | category | flops | bytes accessed | tf_op | source)
XLA Modules:
  0.0 53.2 jit_solution(5941736317005936246)
XLA Ops:
  0.6 49.8 %shard_map.68 = (bf16[4,64,8,128]{3,2,1,0:T(8,128)(2,1)}, bf16[4,64,8,128]{3,2,1,0:T(8,128)(2,1)}) custom-call(bf16[4,64,8,128]{3,2,1,0:T(8,128)(2,1)} %frames_ref.1, s32[3,16]{1,0:T(4,128)} %mf_ref.1, s32[3,16]{1,0:T(4,128)} %mb_ref.1, bf16[2,64,128]{2,1,0:T(8,128)(2,1)} %join_ref.1, bf16[2,4,9,64,64]{4,3,2,1,0:T(8,128)(2,1)} %conv_ref.1), custom_call_target="tpu_custom_call" | custom-call | tf_op jit(solution)/shard_map/pallas_call | solution.py:408
  50.4 0.0 copy-start
  50.4 1.9 %copy.9 = bf16[4,64,8,128]{3,2,1,0:T(8,128)(2,1)} copy(bf16[4,64,8,128]{3,2,1,0:T(8,128)(2,1)} %get-tuple-element.4) | data formatting | bytes 1048576
  52.4 0.0 copy-done
  52.4 0.8 %copy.10 = bf16[4,64,8,128]{3,2,1,0:T(8,128)(2,1)} copy(bf16[4,64,8,128]{3,2,1,0:T(8,128)(2,1)S(1)} %copy-done) | data formatting | bytes 1048576
Async XLA Ops:
  50.4 1.9 %copy-start = (bf16[4,64,8,128]{3,2,1,0:T(8,128)(2,1)S(1)}, bf16[4,64,8,128]{3,2,1,0:T(8,128)(2,1)}, u32[]{:S(2)}) copy-start(bf16[4,64,8,128]{3,2,1,0:T(8,128)(2,1)} %get-tuple-element.5) | copy-start | bytes 1572868

commit v3 on v2

--- a/solution.py
+++ b/solution.py
@@ -119,17 +119,35 @@
         back = frame_count - 2 - step
         mine[frame_count - 1 + step:frame_count + step, 0:bc] = mb_ref[back:back + 1, :]
 
+    identity = (
+        lax.broadcasted_iota(jnp.int32, (channels, channels), 0)
+        == lax.broadcasted_iota(jnp.int32, (channels, channels), 1)
+    ).astype(jnp.bfloat16)
     for d in range(2):
         joined = join_ref[d]
         wj_ref[d, :, :lanes] = blockdiag(joined[:, :channels])
         wj_ref[d, :, lanes:] = blockdiag(joined[:, channels:])
 
         def build_layer(layer, carry):
-            for tap in range(9):
-                down, across = tap // 3, tap % 3
-                wc_ref[
-                    d, layer, across * lanes:(across + 1) * lanes, down * lanes:(down + 1) * lanes
-                ] = blockdiag(conv_ref[d, layer, tap])
+            stacked = conv_ref[d, layer].reshape(9 * channels, channels)
+            turned = matmul_t(identity, stacked).astype(jnp.bfloat16)
+            blank = jnp.zeros((channels, channels), jnp.bfloat16)
+
+            def tap(down, across):
+                start = (3 * down + across) * channels
+                return turned[:, start:start + channels]
+
+            for side in range(2):
+                order = (0, 1, 2, None) if side == 0 else (1, 0, None, 2)
+                depth = (0, 1, 2, None) if side == 0 else (0, 1, None, 2)
+                for k, down in enumerate(depth):
+                    wc_ref[d, layer, side, k * channels:(k + 1) * channels, :] = jnp.concatenate(
+                        [
+                            blank if down is None or across is None else tap(down, across)
+                            for across in order
+                        ],
+                        axis=1,
+                    )
             return carry
 
         lax.fori_loop(0, layers, build_layer, 0)
@@ -239,6 +257,13 @@
         cand[d, index] = tile
         cand[d, kept + index] = pltpu.roll(tile, channels, axis=2)
 
+    def activate(d, slot, start, value):
+        size = value.shape[0]
+        z_ref[d, slot, 0, start:start + size, :] = value.astype(jnp.bfloat16)
+        z_ref[d, slot, 1, start:start + size, :] = pltpu.roll(value, channels, axis=1).astype(
+            jnp.bfloat16
+        )
+
     def begin(d, t):
         @pl.when(t == 0)
         def _():
@@ -275,7 +300,10 @@
             def _():
                 edge_copy(d, t, side, 1 - side).start()
         h_ref[d, halo:halo + own, :] = first
-        z_ref[d, 0, halo:halo + own, :] = leaky(first.astype(jnp.float32)).astype(jnp.bfloat16)
+        activate(d, 0, halo, leaky(first.astype(jnp.float32)))
+
+    top_inside = (me > 0).astype(jnp.float32)
+    bottom_inside = (me < devices - 1).astype(jnp.float32)
 
     def finish(d, t):
         for side in range(2):
@@ -286,58 +314,68 @@
                 edge_copy(d, t, side, side).wait_recv()
                 edge = edge_in[d, t, side]
                 h_ref[d, start:start + halo, :] = edge
-                z_ref[d, 0, start:start + halo, :] = leaky(edge.astype(jnp.float32)).astype(
-                    jnp.bfloat16
-                )
+                activate(d, 0, start, leaky(edge.astype(jnp.float32)))
 
             @pl.when(jnp.logical_not(present(1 if side else -1)))
             def _():
                 h_ref[d, start:start + halo, :] = jnp.zeros((halo, lanes), jnp.bfloat16)
-                z_ref[d, 0, start:start + halo, :] = jnp.zeros((halo, lanes), jnp.bfloat16)
+                for swap in range(2):
+                    z_ref[d, 0, swap, start:start + halo, :] = jnp.zeros(
+                        (halo, lanes), jnp.bfloat16
+                    )
 
         for layer in range(layers):
             out_rows = rows + 2 * (layers - 1 - layer)
             size = out_rows * width
-            source = z_ref.at[d, layer % 2]
-            target = z_ref.at[d, 1 - layer % 2]
-            stack = jnp.concatenate(
-                [source[(layer + k) * width:(layer + k) * width + size, :] for k in range(3)],
-                axis=1,
+            plain = z_ref.at[d, layer % 2, 0]
+            turned = z_ref.at[d, layer % 2, 1]
+            rows0 = pl.ds(layer * width, size)
+            rows1 = pl.ds((layer + 1) * width, size)
+            below = plain[(layer + 2) * width:(layer + 2) * width + size, :]
+            low = lax.broadcasted_iota(jnp.int32, (size, lanes), 1) < channels
+            upper = jnp.where(low, plain[rows0, :], turned[rows1, :])
+            lower = jnp.where(low, turned[rows0, :], plain[rows1, :])
+            one = jnp.dot(
+                jnp.concatenate([upper, below], axis=1), wc_ref[d, layer, 0],
+                preferred_element_type=jnp.float32,
             )
-            summed = matmul_t(stack, wc_ref[d, layer])
+            two = jnp.dot(
+                jnp.concatenate([lower, below], axis=1), wc_ref[d, layer, 1],
+                preferred_element_type=jnp.float32,
+            )
+            tap0 = jnp.where(low, one[:, :lanes], two[:, :lanes])
+            tap1 = pltpu.roll(jnp.where(low, two[:, :lanes], one[:, :lanes]), channels, axis=1)
+            tap2 = jnp.where(low, one[:, lanes:], two[:, lanes:])
             place = lax.broadcasted_iota(jnp.int32, (out_rows, BS, lanes), 1)
             lefts = lax.broadcasted_iota(jnp.int32, (out_rows, BS, lanes), 2) < channels
-            before = pltpu.roll(summed[:, :lanes].reshape(out_rows, width, lanes), 1, axis=1)
+            before = pltpu.roll(tap0.reshape(out_rows, width, lanes), 1, axis=1)
             seam = before[:, :BS]
             crossed = jnp.where(lefts, 0.0, pltpu.roll(seam, channels, axis=2))
             before = jnp.concatenate(
                 [jnp.where(place == 0, crossed, seam), before[:, BS:]], axis=1
             ).reshape(size, lanes)
-            after = pltpu.roll(
-                summed[:, 2 * lanes:].reshape(out_rows, width, lanes), width - 1, axis=1
-            )
+            after = pltpu.roll(tap2.reshape(out_rows, width, lanes), width - 1, axis=1)
             seam = after[:, width - BS:]
             crossed = jnp.where(lefts, pltpu.roll(seam, channels, axis=2), 0.0)
             after = jnp.concatenate(
                 [after[:, :width - BS], jnp.where(place == BS - 1, crossed, seam)], axis=1
             ).reshape(size, lanes)
             base = (layer + 1) * width
-            total = h_ref[d, base:base + size, :].astype(jnp.float32) + summed[:, lanes:2 * lanes]
+            total = h_ref[d, base:base + size, :].astype(jnp.float32) + tap1
             rounded = (total + before + after).astype(jnp.bfloat16)
             if layer < layers - 1:
                 h_ref[d, base:base + size, :] = rounded
-                target[base:base + size, :] = leaky(rounded.astype(jnp.float32)).astype(jnp.bfloat16)
+                active = leaky(rounded.astype(jnp.float32))
                 outside = halo - base
-
-                @pl.when(me == 0)
-                def _():
-                    target[base:halo, :] = jnp.zeros((outside, lanes), jnp.bfloat16)
-
-                @pl.when(me == devices - 1)
-                def _():
-                    target[halo + own:halo + own + outside, :] = jnp.zeros(
-                        (outside, lanes), jnp.bfloat16
-                    )
+                active = jnp.concatenate(
+                    [
+                        active[:outside] * top_inside,
+                        active[outside:size - outside],
+                        active[size - outside:] * bottom_inside,
+                    ],
+                    axis=0,
+                )
+                activate(d, 1 - layer % 2, base, active)
             else:
                 grid = rounded.astype(jnp.float32).reshape(rows, pairs, BS, lanes)
                 for j in range(pairs):
@@ -414,7 +452,7 @@
             pltpu.VMEM((frame_count, own, lanes), jnp.bfloat16),
             pltpu.VMEM((2, channels * rows, cols), jnp.float32),
             pltpu.VMEM((2, lanes, 2 * lanes), jnp.bfloat16),
-            pltpu.VMEM((2, layers, 3 * lanes, 3 * lanes), jnp.bfloat16),
+            pltpu.VMEM((2, layers, 2, 2 * lanes, 2 * lanes), jnp.bfloat16),
             pltpu.VMEM((8, 128), jnp.int32),
             pltpu.VMEM((sides, 8, 128), jnp.int32),
             pltpu.VMEM((sides + 1, 8, 128), jnp.int32),
@@ -424,7 +462,7 @@
             pltpu.VMEM((2, steps, sides, cap // 2 * BS * BS, lanes), jnp.bfloat16),
             pltpu.VMEM((2, rows, width, lanes), jnp.float32),
             pltpu.VMEM((2, own + 2 * halo, lanes), jnp.bfloat16),
-            pltpu.VMEM((2, 2, own + 2 * halo, lanes), jnp.bfloat16),
+            pltpu.VMEM((2, 2, 2, own + 2 * halo, lanes), jnp.bfloat16),
             pltpu.VMEM((2, frame_count, 2, halo, lanes), jnp.bfloat16),
             pltpu.VMEM((2, frame_count, 2, halo, lanes), jnp.bfloat16),
             pltpu.SemaphoreType.DMA((sides,)),

time: 53.3 us -> 51.4 us (0.964)
  Pallas kernels: 49.8 us -> 47.9 us
    pallas_call x1, Pallas kernels: 49.8 us -> 47.9 us  [on_device(): pl.pallas_call(functools.partial(sweep_kernel, dims), out_shape=(result,...]
where the time goes in v3:
time: 51.4 us; the launch traced here: 51.3 us
  Pallas kernels  47.9 us (93%)
  local copies, waits for them, and re-layouts  2.72 us (5%)
  between operations  0.65 us (1%)
    pallas_call x1, Pallas kernels, on_device(): pl.pallas_call(functools.partial(sweep_kernel, dims), out_shape=(result,...  47.9 us
    unnamed x4, local copies, waits for them, and re-layouts  2.72 us

profile of v3, /device:TPU:11, one launch (start us, length us, event | category | flops | bytes accessed | tf_op | source)
XLA Modules:
  0.0 51.3 jit_solution(16125313560533686750)
XLA Ops:
  0.6 47.9 %shard_map.68 = (bf16[4,64,8,128]{3,2,1,0:T(8,128)(2,1)}, bf16[4,64,8,128]{3,2,1,0:T(8,128)(2,1)}) custom-call(bf16[4,64,8,128]{3,2,1,0:T(8,128)(2,1)} %frames_ref.1, s32[3,16]{1,0:T(4,128)} %mf_ref.1, s32[3,16]{1,0:T(4,128)} %mb_ref.1, bf16[2,64,128]{2,1,0:T(8,128)(2,1)} %join_ref.1, bf16[2,4,9,64,64]{4,3,2,1,0:T(8,128)(2,1)} %conv_ref.1), custom_call_target="tpu_custom_call" | custom-call | tf_op jit(solution)/shard_map/pallas_call | solution.py:446
  48.5 0.0 copy-start
  48.5 1.9 %copy.9 = bf16[4,64,8,128]{3,2,1,0:T(8,128)(2,1)} copy(bf16[4,64,8,128]{3,2,1,0:T(8,128)(2,1)} %get-tuple-element.4) | data formatting | bytes 1048576
  50.5 0.0 copy-done
  50.5 0.8 %copy.10 = bf16[4,64,8,128]{3,2,1,0:T(8,128)(2,1)} copy(bf16[4,64,8,128]{3,2,1,0:T(8,128)(2,1)S(1)} %copy-done) | data formatting | bytes 1048576
Async XLA Ops:
  48.5 1.9 %copy-start = (bf16[4,64,8,128]{3,2,1,0:T(8,128)(2,1)S(1)}, bf16[4,64,8,128]{3,2,1,0:T(8,128)(2,1)}, u32[]{:S(2)}) copy-start(bf16[4,64,8,128]{3,2,1,0:T(8,128)(2,1)} %get-tuple-element.5) | copy-start | bytes 1572868

commit v4 on v3

--- a/solution.py
+++ b/solution.py
@@ -128,6 +128,8 @@
         wj_ref[d, :, :lanes] = blockdiag(joined[:, :channels])
         wj_ref[d, :, lanes:] = blockdiag(joined[:, channels:])
 
+
+    def build_weights(d):
         def build_layer(layer, carry):
             stacked = conv_ref[d, layer].reshape(9 * channels, channels)
             turned = matmul_t(identity, stacked).astype(jnp.bfloat16)
@@ -171,7 +173,8 @@
             )
         return carry
 
-    lax.fori_loop(0, frame_count, load_frame, 0)
+    load_frame(0, 0)
+    load_frame(frame_count - 1, 0)
 
     def emit(d, t):
         value = h_ref[d, halo:halo + own, :].astype(jnp.float32).reshape(rows, width, lanes)
@@ -403,6 +406,9 @@
 
         @pl.when(t == 0)
         def _():
+            build_weights(0)
+            build_weights(1)
+            lax.fori_loop(1, frame_count - 1, load_frame, 0)
             build_tables()
 
         finish(0, t)

time: 51.4 us -> 51.5 us (level)
  no operation moved by 1% of the time
where the time goes in v4:
time: 51.5 us; the launch traced here: 51.3 us
  Pallas kernels  47.9 us (93%)
  local copies, waits for them, and re-layouts  2.72 us (5%)
  between operations  0.65 us (1%)
    pallas_call x1, Pallas kernels, on_device(): pl.pallas_call(functools.partial(sweep_kernel, dims), out_shape=(result,...  47.9 us
    unnamed x4, local copies, waits for them, and re-layouts  2.72 us

profile of v4, /device:TPU:11, one launch (start us, length us, event | category | flops | bytes accessed | tf_op | source)
XLA Modules:
  0.0 51.3 jit_solution(5812588042531576702)
XLA Ops:
  0.6 47.9 %shard_map.68 = (bf16[4,64,8,128]{3,2,1,0:T(8,128)(2,1)}, bf16[4,64,8,128]{3,2,1,0:T(8,128)(2,1)}) custom-call(bf16[4,64,8,128]{3,2,1,0:T(8,128)(2,1)} %frames_ref.1, s32[3,16]{1,0:T(4,128)} %mf_ref.1, s32[3,16]{1,0:T(4,128)} %mb_ref.1, bf16[2,64,128]{2,1,0:T(8,128)(2,1)} %join_ref.1, bf16[2,4,9,64,64]{4,3,2,1,0:T(8,128)(2,1)} %conv_ref.1), custom_call_target="tpu_custom_call" | custom-call | tf_op jit(solution)/shard_map/pallas_call | solution.py:452
  48.6 0.0 copy-start
  48.6 1.9 %copy.9 = bf16[4,64,8,128]{3,2,1,0:T(8,128)(2,1)} copy(bf16[4,64,8,128]{3,2,1,0:T(8,128)(2,1)} %get-tuple-element.4) | data formatting | bytes 1048576
  50.5 0.0 copy-done
  50.5 0.8 %copy.10 = bf16[4,64,8,128]{3,2,1,0:T(8,128)(2,1)} copy(bf16[4,64,8,128]{3,2,1,0:T(8,128)(2,1)S(1)} %copy-done) | data formatting | bytes 1048576
Async XLA Ops:
  48.6 1.9 %copy-start = (bf16[4,64,8,128]{3,2,1,0:T(8,128)(2,1)S(1)}, bf16[4,64,8,128]{3,2,1,0:T(8,128)(2,1)}, u32[]{:S(2)}) copy-start(bf16[4,64,8,128]{3,2,1,0:T(8,128)(2,1)} %get-tuple-element.5) | copy-start | bytes 1572868
